TPU v7x, 512 devices: a whole 4x4x16 slice. The times are simulated.
512 devices in a mesh: ctx: 16 (over z), ch: 32 (over x, y, core).
Axes of the slice: x: 4, y: 4, z: 16, core: 2. Of those that a mesh axis runs over, the one named last changes fastest.
Arguments:
- features: bfloat16 [2, 16, 128, 3, 4096], P(None, 'ctx', None, None, 'ch'), may hold values from -6 to 6
- short_weight: bfloat16 [7, 3, 4096], P(None, None, 'ch'), may hold values from -2 to 2
- long_filter: bfloat16 [2, 16, 128, 4096], P(None, 'ctx', None, 'ch'), may hold values from -0.125 to 0.125
- skip_gain: float32 [4096], P('ch'), may hold values from -4 to 4
- out_weight: bfloat16 [4096, 4096], P('ch'), may hold values from -0.1875 to 0.1875
Outputs:
- mixed: bfloat16 [2, 16, 128, 4096], P(None, 'ctx', None, 'ch')
All inputs are finite; a program needn't handle non-finite values.
Results may differ from a plain program's by a relative error of at most 0.015.
Values may be sent and summed in bfloat16 or wider, within the bound.
No kernel may reach another device: no remote copies, remote signals or barrier semaphores. Data moves between devices by JAX's collectives and lax.ppermute only.
A program may use at most 64 MiB of HBM per device.

v0:
```python
import math
import jax
import jax.numpy as jnp
from jax import lax
from jax.sharding import PartitionSpec as P


def from_behind(value, axis, steps):
    count = lax.axis_size(axis)
    initial, last = (max(0, -steps), min(count, count - steps))
    return lax.ppermute(value, axis, [(source, source + steps) for source in range(initial, last)])


def transform_tables(length):
    period = 2 * length
    indices = jnp.arange(period, dtype=jnp.int32)
    phases = indices[:, None] * indices[None, :] % period
    angles = phases.astype(jnp.float32) * (2.0 * math.pi / period)
    cosine = jnp.cos(angles)
    sine_table = jnp.sin(angles)
    forward_full = jnp.concatenate([cosine, -sine_table], axis=0)
    forward_data = forward_full[:, :length]
    inverse = jnp.concatenate([cosine[:length], -sine_table[:length]], axis=1) / period
    return (forward_full, forward_data, inverse)


def complex_product(first, second):
    middle = first.shape[-2] // 2
    real_a = first[..., :middle, :]
    imag_a = first[..., middle:, :]
    real_b = second[..., :middle, :]
    imag_b = second[..., middle:, :]
    return jnp.concatenate(
        [real_a * real_b - imag_a * imag_b, real_a * imag_b + imag_a * real_b], axis=-2
    )


def featurize(tokens, before, kernel):
    extended = jnp.concatenate([before, tokens], axis=0).astype(jnp.float32)
    length = tokens.shape[0]
    margin_rows = kernel.shape[0] - 1
    summed = jnp.zeros(tokens.shape, jnp.float32)
    for offset in range(kernel.shape[0]):
        summed = (
            summed
            + kernel[offset].astype(jnp.float32)
            * extended[margin_rows - offset : margin_rows - offset + length]
        )
    return summed


def ordered(blocks):
    return jnp.concatenate([blocks[0], jnp.flip(blocks[1], axis=0)], axis=0)


def local(features, short_weight, long_filter, skip_gain, out_weight):
    pair_count = lax.axis_size("ctx")
    blocks_all = 2 * pair_count
    position = lax.axis_index("ctx")
    length = features.shape[2]
    margin_rows = short_weight.shape[0] - 1
    trailing = features[:, 0, length - margin_rows :]
    from_before = from_behind(trailing[0], "ctx", 1)
    from_after = from_behind(trailing[1], "ctx", -1)
    second_rim = jnp.where(position == pair_count - 1, trailing[0], from_after)
    first_feat = featurize(features[0, 0], from_before, short_weight)
    second_feat = featurize(features[1, 0], second_rim, short_weight)
    featured = jnp.stack([first_feat, second_feat], axis=0)
    queries = featured[:, :, 0]
    gated_keys = (featured[:, :, 1] * featured[:, :, 2]).astype(jnp.bfloat16)
    forward_full, forward_data, inverse = transform_tables(length)
    precise = lax.Precision.HIGHEST
    gathered = lax.all_gather(long_filter, "ctx", axis=1, tiled=True)
    lag_order = ordered(gathered)
    padded = jnp.concatenate(
        [jnp.zeros((1,) + lag_order.shape[1:], lag_order.dtype), lag_order], axis=0
    )
    lag_spectra = jnp.einsum(
        "fn,knc->kfc", forward_data, padded.astype(jnp.float32), precision=precise
    )
    frequency = jnp.arange(4 * length, dtype=jnp.int32) % (2 * length)
    parity = jnp.where(frequency % 2 == 0, 1.0, -1.0).astype(jnp.float32)[:, None]
    responses = lag_spectra[1:] + parity * lag_spectra[:-1]
    targets = jnp.stack([position, blocks_all - 1 - position])

    def absorb(totals, spectrum, source):
        for target_slot in range(2):
            distance = targets[target_slot] - source
            clamped = jnp.maximum(distance, 0)
            response = lax.dynamic_index_in_dim(responses, clamped, 0, keepdims=False)
            contribution = complex_product(response, spectrum)
            totals = totals.at[target_slot].add(jnp.where(distance >= 0, contribution, 0.0))
        return totals

    zeroed = jnp.zeros((2, 4 * length, gated_keys.shape[-1]), jnp.float32)

    def transform_block(values):
        return jnp.dot(forward_data, values.astype(jnp.float32), precision=precise)

    totals = zeroed
    shards = lax.all_gather(gated_keys[:, None], "ctx", axis=1, tiled=True)

    def advance(running, offset):
        couple = lax.dynamic_index_in_dim(shards, offset, 1, keepdims=False)
        running = absorb(running, transform_block(couple[0]), offset)
        running = absorb(running, transform_block(couple[1]), blocks_all - 1 - offset)
        return (running, None)

    totals, unused = lax.scan(advance, totals, jnp.arange(shards.shape[1], dtype=jnp.int32))
    convolved = jnp.einsum("tf,hfc->htc", inverse, totals, precision=precise)
    activated = (queries * (convolved + skip_gain * gated_keys.astype(jnp.float32))).astype(
        jnp.bfloat16
    )
    token_rows = activated.reshape(2 * length, activated.shape[-1])
    channels = token_rows.shape[1]
    owned = lax.psum_scatter(
        lax.dot_general(
            out_weight, token_rows, (((0,), (1,)), ((), ())), preferred_element_type=jnp.float32
        ).astype(jnp.bfloat16),
        "ch",
        scatter_dimension=0,
        tiled=True,
    ).astype(jnp.float32)
    result = owned.T
    return result.astype(jnp.bfloat16).reshape(2, 1, length, channels)


def solution(mesh):
    in_specs = (
        P(None, "ctx", None, None, "ch"),
        P(None, None, "ch"),
        P(None, "ctx", None, "ch"),
        P("ch"),
        P("ch", None),
    )
    out_specs = P(None, "ctx", None, "ch")
    return jax.shard_map(local, mesh=mesh, in_specs=in_specs, out_specs=out_specs, check_vma=False)
```

profile of v0, /device:TPU:2, one launch (start us, length us, event | category | flops | bytes accessed | tf_op | source)
XLA Modules:
  0.0 414.9 jit_solution(9419086972166073403)
XLA Ops:
  6.5 1.7 copy.15
  9.0 3.8 collective-permute-start
  12.8 1.3 collective-permute-start.1
  16.1 2.2 collective-permute-done.1
  22.3 62.3 %all-gather.4.cloned.1.call-done = bf16[2,16,128,128]{2,3,1,0:T(8,128)(2,1)} async-done(((bf16[2,1,128,128]{2,3,1,0:T(8,128)(2,1)}), bf16[2,16,128,128]{2,3,1,0:T(8,128)(2,1)}) %all-gather.4.cloned.1.call-update) | async-done | bytes 1048592 | tf_op jit(solution)/shard_map/all_gather | solution.py:73
  84.6 1.3 slice_bitcast_fusion.1
  85.9 3.7 convolution_bitcast_fusion.2
  89.6 4.5 %fusion.7 = f32[32,512,128]{1,2,0:T(8,128)} fusion(f32[33,512,128]{1,2,0:T(8,128)S(1)} %convolution_bitcast_fusion.2, f32[512]{0:T(512)S(1)} %fusion.56), kind=kLoop, calls=%fused_computation.35 | loop fusion | flops 4194304 | bytes 25167872 | tf_op jit(solution)/shard_map/add | solution.py:83
  94.2 60.3 %all-gather.6.cloned.1.call-done = bf16[2,2048,1,128]{3,1,0,2:T(8,128)(2,1)} async-done(((bf16[2,128,1,128]{3,1,0,2:T(8,128)(2,1)}), bf16[2,2048,1,128]{3,1,0,2:T(8,128)(2,1)}) %all-gather.6.cloned.1.call-update) | async-done | bytes 1048592 | tf_op jit(solution)/shard_map/all_gather | solution.py:101
  154.5 149.5 %while.16 = (s32[]{:T(128)}, f32[2,512,128]{1,2,0:T(8,128)S(1)}, s32[16]{0:T(128)S(1)}, s32[]{:T(128)}, f32[32,512,128]{1,2,0:T(8,128)}, /*index=5*/bf16[2,16,12...) while((s32[]{:T(128)}, f32[2,512,128]{1,2,0:T(8,128)S(1)}, ...), condition=%wide.region_1.2_spmd, body=%wide.region_0.1_spmd.sunk | while | flops 202899456 | bytes 6881675 | solution.py:109
  159.5 1.2 subtract_bitcast_fusion.6
  161.4 1.1 convolution_bitcast_fusion.7
  162.5 1.2 subtract_bitcast_fusion.7
  168.8 1.2 subtract_bitcast_fusion.6
  170.8 1.1 convolution_bitcast_fusion.7
  171.9 1.2 subtract_bitcast_fusion.7
  178.1 1.2 subtract_bitcast_fusion.6
  180.1 1.1 convolution_bitcast_fusion.7
  181.2 1.2 subtract_bitcast_fusion.7
  187.5 1.2 subtract_bitcast_fusion.6
  189.5 1.1 convolution_bitcast_fusion.7
  190.6 1.2 subtract_bitcast_fusion.7
  196.8 1.2 subtract_bitcast_fusion.6
  198.8 1.1 convolution_bitcast_fusion.7
  199.9 1.2 subtract_bitcast_fusion.7
  206.2 1.2 subtract_bitcast_fusion.6
  208.2 1.1 convolution_bitcast_fusion.7
  209.3 1.2 subtract_bitcast_fusion.7
  215.5 1.2 subtract_bitcast_fusion.6
  217.5 1.1 convolution_bitcast_fusion.7
  218.6 1.2 subtract_bitcast_fusion.7
  224.9 1.2 subtract_bitcast_fusion.6
  226.9 1.1 convolution_bitcast_fusion.7
  227.9 1.2 subtract_bitcast_fusion.7
  234.2 1.2 subtract_bitcast_fusion.6
  236.2 1.1 convolution_bitcast_fusion.7
  237.3 1.2 subtract_bitcast_fusion.7
  243.6 1.2 subtract_bitcast_fusion.6
  245.5 1.1 convolution_bitcast_fusion.7
  246.6 1.2 subtract_bitcast_fusion.7
  252.9 1.2 subtract_bitcast_fusion.6
  254.9 1.1 convolution_bitcast_fusion.7
  256.0 1.2 subtract_bitcast_fusion.7
  260.5 1.1 convolution_bitcast_fusion.6
  262.2 1.2 subtract_bitcast_fusion.6
  264.2 1.1 convolution_bitcast_fusion.7
  265.3 1.2 subtract_bitcast_fusion.7
  269.9 1.1 convolution_bitcast_fusion.6
  271.6 1.2 subtract_bitcast_fusion.6
  273.6 1.1 convolution_bitcast_fusion.7
  274.7 1.2 subtract_bitcast_fusion.7
  280.9 1.2 subtract_bitcast_fusion.6
  282.9 1.1 convolution_bitcast_fusion.7
  284.0 1.2 subtract_bitcast_fusion.7
  288.5 1.1 convolution_bitcast_fusion.6
  290.3 1.2 subtract_bitcast_fusion.6
  292.3 1.1 convolution_bitcast_fusion.7
  293.4 1.2 subtract_bitcast_fusion.7
  299.6 1.2 subtract_bitcast_fusion.6
  301.6 1.1 convolution_bitcast_fusion.7
  302.7 1.2 subtract_bitcast_fusion.7
  305.4 2.5 copy.19
  308.0 98.9 %reduce-scatter.4.cloned.1.call-done = bf16[128,256]{1,0:T(8,128)(2,1)} async-done(((bf16[4096,256]{1,0:T(8,128)(2,1)}), bf16[128,256]{1,0:T(8,128)(2,1)}) %reduce-scatter.4.cloned.1.call-update) | async-done | bytes 65552
  406.8 1.6 copy.20
  (131 shorter events, 35.9 us)
Async XLA Ops:
  6.5 298.2 %copy-start = (bf16[128,4096]{1,0:T(8,128)(2,1)S(1)}, bf16[128,4096]{1,0:T(8,128)(2,1)}, u32[]{:S(2)}) copy-start(bf16[128,4096]{1,0:T(8,128)(2,1)} %param.19) | copy-start | bytes 3145732
  6.5 78.1 %all-gather.4.cloned.1.call-start = ((), (), s32[]{:S(2)}) async-start(), calls=%async_computation.1 | async-start | bytes 1114112 | tf_op jit(solution)/shard_map/all_gather | solution.py:73
  8.2 146.2 %all-gather.6.cloned.1.call-start = ((), (), s32[]{:S(2)}) async-start(), calls=%async_computation.2 | async-start | bytes 1114112 | tf_op jit(solution)/shard_map/all_gather | solution.py:101
  9.0 10.1 %collective-permute-start = (bf16[6,3,128]{2,0,1:T(8,128)(2,1)S(1)}, bf16[6,3,128]{2,0,1:T(8,128)(2,1)S(1)}, u32[]{:S(2)}, u32[]{:S(2)}) collective-permute-start(bf16[6,3,128]{2,0,1:T(8,128)(2,1)S(1)} %get-tuple-element.184), channel_id=1, source_target_pairs={{0,32},{32,64},{64,96},{96,128},{128,160},{160,192},{192,224},{224... | collective-permute-start | bytes 13832 | tf_op jit(solution)/shard_map/ppermute | solution.py:11
  12.8 5.5 %collective-permute-start.1 = (bf16[6,3,128]{2,0,1:T(8,128)(2,1)S(1)}, bf16[6,3,128]{2,0,1:T(8,128)(2,1)S(1)}, u32[]{:S(2)}, u32[]{:S(2)}) collective-permute-start(bf16[6,3,128]{2,0,1:T(8,128)(2,1)S(1)} %get-tuple-element.183), channel_id=1, source_target_pairs={{32,0},{64,32},{96,64},{128,96},{160,128},{192,160},{224,192},{256... | collective-permute-start | bytes 13832 | tf_op jit(solution)/shard_map/ppermute | solution.py:11
  20.1 386.7 %reduce-scatter.4.cloned.1.call-start = ((), (), s32[]{:S(2)}) async-start(), calls=%async_computation.3 | async-start | bytes 2162688
  154.5 149.5 %copy-start.1 = (bf16[2,128,1,128]{3,1,0,2:T(8,128)(2,1)S(1)}, bf16[2,128,1,128]{3,1,0,2:T(8,128)(2,1)}, u32[]{:S(2)}) copy-start(bf16[2,128,1,128]{3,1,0,2:T(8,128)(2,1)} %fusion.44) | copy-start | bytes 196612
  154.5 149.5 %copy-start.2 = (f32[128]{0:T(128)S(1)}, f32[128]{0:T(128)}, u32[]{:S(2)}) copy-start(f32[128]{0:T(128)} %param.18) | copy-start | bytes 1540
Sparse Core Ops, SparseCore 0:
  9.4 75.1 all-gather.3
  86.7 67.7 all-gather.5
  308.1 98.7 reduce-scatter.3
where the time goes:
time: 419 us; the launch traced here: 415 us
  waiting for transfers between devices  224 us (53%)
  loops' own time  64 us (15%)
  other arithmetic  51 us (12%)
  matrix products  39.4 us (9%)
  local copies, waits for them, and re-layouts  18.2 us (4%)
  between operations  13.3 us (3%)
  starting transfers between devices  5.19 us (1%)
    unnamed x4, waiting for transfers between devices  98.9 us
    another operation x1, loops' own time, local(): lax.scan(advance, totals, jnp.arange(shards.shape[1], dtype=jnp.int32))  64 us
    all_gather x1, waiting for transfers between devices, local(): gathered = lax.all_gather(long_filter, 'ctx', axis=1, tiled=True)  62.3 us
    all_gather x1, waiting for transfers between devices, local(): shards = lax.all_gather(gated_keys[:, None], 'ctx', axis=1, tiled=True)  60.3 us
    concatenate x32, other arithmetic, complex_product(): jnp.concatenate([real_a * real_b - imag_a * imag_b, real_a * imag_b + ima...  37.2 us
    dot_general x32, matrix products, transform_block(): return jnp.dot(forward_data, values.astype(jnp.float32), precision=precise)  34.4 us
    dynamic_slice x16, local copies, waits for them, and re-layouts, local(): lax.scan(advance, totals, jnp.arange(shards.shape[1], dtype=jnp.int32))  9.38 us
  transfers between devices with their start and end apart: 5, of which 4 were waited for; matrix products, arithmetic and copies ran while one was open for 4% of the time, Pallas kernels for 0%

commit v1 on v0

--- a/solution.py
+++ b/solution.py
@@ -98,7 +98,9 @@
         return jnp.dot(forward_data, values.astype(jnp.float32), precision=precise)
 
     totals = zeroed
-    shards = lax.all_gather(gated_keys[:, None], "ctx", axis=1, tiled=True)
+    shards = jnp.concatenate(
+        lax.all_to_all(jnp.stack([gated_keys[:, None]] * lax.axis_size("ctx")), "ctx", 0, 0), axis=1
+    )
 
     def advance(running, offset):
         couple = lax.dynamic_index_in_dim(shards, offset, 1, keepdims=False)

time: 419 us -> 385 us (0.919)
  waiting for transfers between devices: 224 us -> 180 us
  matrix products: 39.4 us -> 16.4 us
  local copies, waits for them, and re-layouts: 18.2 us -> 34.6 us
  starting transfers between devices: 5.19 us -> 21.2 us
    all_gather x1 -> x0, waiting for transfers between devices: 60.3 us -> none  [local(): shards = lax.all_gather(gated_keys[:, None], 'ctx', axis=1, tiled=True)]
    dot_general x32, matrix products: 34.4 us -> 10.1 us  [transform_block(): return jnp.dot(forward_data, values.astype(jnp.float32), precision=precise)]
    all_gather x1, waiting for transfers between devices: 62.3 us -> 80.4 us  [local(): gathered = lax.all_gather(long_filter, 'ctx', axis=1, tiled=True)]
    all_to_all x0 -> x1, starting transfers between devices: none -> 15.2 us  [local(): lax.all_to_all(jnp.stack([gated_keys[:, None]] * lax.axis_size('ctx')), '...]
    dynamic_slice x0 -> x16, local copies, waits for them, and re-layouts: none -> 13.6 us  [advance(): couple = lax.dynamic_index_in_dim(shards, offset, 1, keepdims=False)]
    unnamed x4 -> x3, waiting for transfers between devices: 98.9 us -> 100 us
  transfers between devices with their start and end apart: 5 -> 5, of which waited for: 4 -> 2; matrix products, arithmetic and copies ran while one was open for 4% -> 5% of each run, Pallas kernels for 0% -> 0%
where the time goes in v1:
time: 385 us; the launch traced here: 382 us
  waiting for transfers between devices  180 us (47%)
  loops' own time  64 us (17%)
  other arithmetic  52 us (14%)
  local copies, waits for them, and re-layouts  34.6 us (9%)
  starting transfers between devices  21.2 us (6%)
  matrix products  16.4 us (4%)
  between operations  13.7 us (4%)
    unnamed x3, waiting for transfers between devices  100 us
    all_gather x1, waiting for transfers between devices, local(): gathered = lax.all_gather(long_filter, 'ctx', axis=1, tiled=True)  80.4 us
    another operation x1, loops' own time, local(): lax.scan(advance, totals, jnp.arange(shards.shape[1], dtype=jnp.int32))  64 us
    concatenate x32, other arithmetic, complex_product(): jnp.concatenate([real_a * real_b - imag_a * imag_b, real_a * imag_b + ima...  37.2 us
    all_to_all x1, starting transfers between devices, local(): lax.all_to_all(jnp.stack([gated_keys[:, None]] * lax.axis_size('ctx')), '...  15.2 us
    dynamic_slice x16, local copies, waits for them, and re-layouts, advance(): couple = lax.dynamic_index_in_dim(shards, offset, 1, keepdims=False)  13.6 us
    dot_general x32, matrix products, transform_block(): return jnp.dot(forward_data, values.astype(jnp.float32), precision=precise)  10.1 us
    dynamic_slice x16, local copies, waits for them, and re-layouts, local(): lax.scan(advance, totals, jnp.arange(shards.shape[1], dtype=jnp.int32))  9.38 us
  transfers between devices with their start and end apart: 5, of which 2 were waited for; matrix products, arithmetic and copies ran while one was open for 5% of the time, Pallas kernels for 0%

profile of v1, /device:TPU:2, one launch (start us, length us, event | category | flops | bytes accessed | tf_op | source)
XLA Modules:
  0.0 382.3 jit_solution(3466336878888789597)
XLA Ops:
  7.3 1.3 collective-permute-start.1
  8.6 4.5 %collective-permute-start = (bf16[6,3,128]{2,0,1:T(8,128)(2,1)S(1)}, bf16[6,3,128]{2,0,1:T(8,128)(2,1)S(1)}, u32[]{:S(2)}, u32[]{:S(2)}) collective-permute-start(bf16[6,3,128]{2,0,1:T(8,128)(2,1)S(1)} %get-tuple-element.191), channel_id=1, source_target_pairs={{0,32},{32,64},{64,96},{96,128},{128,160},{160,192},{192,224},{224... | collective-permute-start | bytes 13832 | tf_op jit(solution)/shard_map/ppermute | solution.py:11
  13.2 1.0 slice_bitcast_fusion.7
  14.1 1.0 slice_convert_fusion.6
  16.3 1.2 stack.15
  17.6 15.2 %all-to-all-start = ((bf16[16,2,1,128,128]{4,3,1,2,0:T(8,128)(2,1)}), bf16[16,2,1,128,128]{4,3,1,2,0:T(8,128)(2,1)}, u32[]{:S(2)}, u32[]{:S(2)}) async-start(bf16[16,2,1,128,128]{4,3,1,2,0:T(8,128)(2,1)} %stack.15), calls=%async_computation | async-start | bytes 2097152 | tf_op jit(solution)/shard_map/all_to_all | solution.py:102
  32.9 1.6 copy.15
  34.5 1.0 fusion.47
  35.5 1.0 fusion.48
  36.5 1.0 fusion.46
  38.2 80.4 %all-gather.2.cloned.1.call-done = bf16[2,16,128,128]{2,3,1,0:T(8,128)(2,1)} async-done(((bf16[2,1,128,128]{2,3,1,0:T(8,128)(2,1)}), bf16[2,16,128,128]{2,3,1,0:T(8,128)(2,1)}) %all-gather.2.cloned.1.call-update) | async-done | bytes 1048592 | tf_op jit(solution)/shard_map/all_gather | solution.py:73
  118.6 1.3 slice_bitcast_fusion.5
  119.9 3.7 convolution_bitcast_fusion.2
  123.6 4.5 %fusion.5 = f32[32,512,128]{1,2,0:T(8,128)} fusion(f32[33,512,128]{1,2,0:T(8,128)S(1)} %convolution_bitcast_fusion.2, f32[512]{0:T(512)S(1)} %fusion.55), kind=kLoop, calls=%fused_computation.34 | loop fusion | flops 4194304 | bytes 25167872 | tf_op jit(solution)/shard_map/add | solution.py:83
  128.3 138.8 %while.16 = (s32[]{:T(128)}, f32[2,512,128]{1,2,0:T(8,128)S(1)}, s32[16]{0:T(128)S(1)}, s32[]{:T(128)}, f32[32,512,128]{1,2,0:T(8,128)}, /*index=5*/bf16[2,16,12...) while((s32[]{:T(128)}, f32[2,512,128]{1,2,0:T(8,128)S(1)}, ...), condition=%wide.region_1.2_spmd, body=%wide.region_0.1_spmd.sunk | while | flops 202899456 | bytes 7012719 | solution.py:111
  131.5 0.8 dynamic-slice_bitcast_fusion.10
  133.3 1.2 subtract_bitcast_fusion.6
  135.6 1.2 subtract_bitcast_fusion.7
  140.1 0.8 dynamic-slice_bitcast_fusion.10
  142.0 1.2 subtract_bitcast_fusion.6
  144.3 1.2 subtract_bitcast_fusion.7
  148.8 0.8 dynamic-slice_bitcast_fusion.10
  150.6 1.2 subtract_bitcast_fusion.6
  153.0 1.2 subtract_bitcast_fusion.7
  157.5 0.8 dynamic-slice_bitcast_fusion.10
  159.3 1.2 subtract_bitcast_fusion.6
  161.6 1.2 subtract_bitcast_fusion.7
  166.2 0.8 dynamic-slice_bitcast_fusion.10
  168.0 1.2 subtract_bitcast_fusion.6
  170.3 1.2 subtract_bitcast_fusion.7
  174.8 0.8 dynamic-slice_bitcast_fusion.10
  176.7 1.2 subtract_bitcast_fusion.6
  179.0 1.2 subtract_bitcast_fusion.7
  183.5 0.8 dynamic-slice_bitcast_fusion.10
  185.3 1.2 subtract_bitcast_fusion.6
  187.7 1.2 subtract_bitcast_fusion.7
  194.0 1.2 subtract_bitcast_fusion.6
  196.3 1.2 subtract_bitcast_fusion.7
  200.9 0.8 dynamic-slice_bitcast_fusion.10
  202.7 1.2 subtract_bitcast_fusion.6
  205.0 1.2 subtract_bitcast_fusion.7
  211.4 1.2 subtract_bitcast_fusion.6
  213.7 1.2 subtract_bitcast_fusion.7
  218.2 0.8 dynamic-slice_bitcast_fusion.10
  220.1 1.2 subtract_bitcast_fusion.6
  222.4 1.2 subtract_bitcast_fusion.7
  228.7 1.2 subtract_bitcast_fusion.6
  231.1 1.2 subtract_bitcast_fusion.7
  235.6 0.8 dynamic-slice_bitcast_fusion.10
  237.4 1.2 subtract_bitcast_fusion.6
  239.7 1.2 subtract_bitcast_fusion.7
  244.3 0.8 dynamic-slice_bitcast_fusion.10
  246.1 1.2 subtract_bitcast_fusion.6
  248.4 1.2 subtract_bitcast_fusion.7
  252.9 0.8 dynamic-slice_bitcast_fusion.10
  254.8 1.2 subtract_bitcast_fusion.6
  257.1 1.2 subtract_bitcast_fusion.7
  261.6 0.8 dynamic-slice_bitcast_fusion.10
  263.4 1.2 subtract_bitcast_fusion.6
  265.8 1.2 subtract_bitcast_fusion.7
  267.8 2.0 fusion.6
  269.8 4.1 %copy.20 = bf16[4096,256]{1,0:T(8,128)(2,1)} copy(bf16[4096,256]{0,1:T(8,128)(2,1)} %fusion.6) | data formatting | bytes 4194304
  273.9 100.0 %reduce-scatter.4.cloned.1.call-done = bf16[128,256]{1,0:T(8,128)(2,1)} async-done(((bf16[4096,256]{1,0:T(8,128)(2,1)}), bf16[128,256]{1,0:T(8,128)(2,1)}) %reduce-scatter.4.cloned.1.call-update) | async-done | bytes 65552
  373.9 1.6 copy.21
  (155 shorter events, 30.0 us)
Async XLA Ops:
  6.5 261.3 %copy-start = (bf16[128,4096]{1,0:T(8,128)(2,1)S(1)}, bf16[128,4096]{1,0:T(8,128)(2,1)}, u32[]{:S(2)}) copy-start(bf16[128,4096]{1,0:T(8,128)(2,1)} %param.19) | copy-start | bytes 3145732
  7.3 7.8 %collective-permute-start.1 = (bf16[6,3,128]{2,0,1:T(8,128)(2,1)S(1)}, bf16[6,3,128]{2,0,1:T(8,128)(2,1)S(1)}, u32[]{:S(2)}, u32[]{:S(2)}) collective-permute-start(bf16[6,3,128]{2,0,1:T(8,128)(2,1)S(1)} %get-tuple-element.192), channel_id=1, source_target_pairs={{32,0},{64,32},{96,64},{128,96},{160,128},{192,160},{224,192},{256... | collective-permute-start | bytes 13832 | tf_op jit(solution)/shard_map/ppermute | solution.py:11
  8.6 7.5 %collective-permute-start = (bf16[6,3,128]{2,0,1:T(8,128)(2,1)S(1)}, bf16[6,3,128]{2,0,1:T(8,128)(2,1)S(1)}, u32[]{:S(2)}, u32[]{:S(2)}) collective-permute-start(bf16[6,3,128]{2,0,1:T(8,128)(2,1)S(1)} %get-tuple-element.191), channel_id=1, source_target_pairs={{0,32},{32,64},{64,96},{96,128},{128,160},{160,192},{192,224},{224... | collective-permute-start | bytes 13832 | tf_op jit(solution)/shard_map/ppermute | solution.py:11
  16.3 20.2 %copy-start.2 = (bf16[2,128,128]{2,1,0:T(8,128)(2,1)}, bf16[2,128,128]{2,1,0:T(8,128)(2,1)S(1)}, u32[]{:S(2)}) copy-start(bf16[2,128,128]{2,1,0:T(8,128)(2,1)S(1)} %fusion.49) | copy-start | bytes 196612
  17.6 110.6 %all-to-all-start = ((bf16[16,2,1,128,128]{4,3,1,2,0:T(8,128)(2,1)}), bf16[16,2,1,128,128]{4,3,1,2,0:T(8,128)(2,1)}, u32[]{:S(2)}, u32[]{:S(2)}) async-start(bf16[16,2,1,128,128]{4,3,1,2,0:T(8,128)(2,1)} %stack.15), calls=%async_computation | async-start | bytes 2097152 | tf_op jit(solution)/shard_map/all_to_all | solution.py:102
  32.8 85.8 %all-gather.2.cloned.1.call-start = ((), (), s32[]{:S(2)}) async-start(), calls=%async_computation.2 | async-start | bytes 1114112 | tf_op jit(solution)/shard_map/all_gather | solution.py:73
  34.5 339.4 %reduce-scatter.4.cloned.1.call-start = ((), (), s32[]{:S(2)}) async-start(), calls=%async_computation.3 | async-start | bytes 2162688
  35.5 92.7 %copy-start.1 = (f32[256,256]{1,0:T(8,128)}, f32[256,256]{1,0:T(8,128)S(1)}, u32[]{:S(2)}) copy-start(f32[256,256]{1,0:T(8,128)S(1)} %fusion.47) | copy-start | bytes 786436
  128.2 138.9 %slice-start = ((f32[256,256]{1,0:T(8,128)}), f32[128,256]{1,0:T(8,128)S(1)}, s32[]{:S(2)}) async-start(f32[256,256]{1,0:T(8,128)} %copy-done.1), calls=%async_computation.4 | async-start | bytes 262144 | tf_op jit(solution)/shard_map/slice | solution.py:23
  128.2 138.9 %copy-start.3 = (bf16[2,128,128]{2,1,0:T(8,128)(2,1)S(1)}, bf16[2,128,128]{2,1,0:T(8,128)(2,1)}, u32[]{:S(2)}) copy-start(bf16[2,128,128]{2,1,0:T(8,128)(2,1)} %copy-done.2) | copy-start | bytes 196612
  128.3 138.9 %copy-start.4 = (f32[128,256]{1,0:T(8,128)S(1)}, f32[128,256]{1,0:T(8,128)}, u32[]{:S(2)}) copy-start(f32[128,256]{1,0:T(8,128)} %slice_negate_fusion) | copy-start | bytes 393220
  128.3 138.9 %copy-start.5 = (f32[128]{0:T(128)S(1)}, f32[128]{0:T(128)}, u32[]{:S(2)}) copy-start(f32[128]{0:T(128)} %param.18) | copy-start | bytes 1540
Sparse Core Ops, SparseCore 0:
  35.7 82.8 all-gather.1
  274.0 99.8 reduce-scatter.3
